TPU v7x, 128 devices: a whole 4x4x4 slice. The times are simulated.
128 devices in a mesh: dp: 32 (over x, z, y_hi), mp: 4 (over y_lo, core).
Axes of the slice: x: 4, y: 4 (y_hi: 2, y_lo: 2; y = y_hi * 2 + y_lo), z: 4, core: 2. Of those that a mesh axis runs over, the one named last changes fastest.
Arguments:
- activations: bfloat16 [32768, 8192], P('dp', 'mp'), may hold values from -6 to 6
- cot_true: bfloat16 [32768, 1024], P('dp', 'mp'), may hold values from -6 to 6
- cot_sampled: bfloat16 [32768, 1024], P('dp', 'mp'), may hold values from -6 to 6
- tile_mask: int32 [64, 8], replicated, may hold values from 0 to 1, as said below
- moment: float32 [8192, 1024], P('dp', 'mp'), may hold values from -0.0012207031 to 0.0012207031
- curvature: float32 [8192, 1024], P('dp', 'mp'), may hold values from 0.003 to 3
Outputs:
- update: float32 [8192, 1024], P('dp', 'mp')
- new_curvature: float32 [8192, 1024], P('dp', 'mp')
Inputs may be any that keep to these rules, and one draw needn't show every extreme that they name: Every column of tile_mask holds exactly 16 ones.
All inputs are finite; a program needn't handle non-finite values.
Results may differ from a plain program's by a relative error of at most 0.0003.
Values may be sent and summed in bfloat16 or wider, within the bound.
A program may use at most 128 MiB of HBM per device.

v0:
```python
import jax
import jax.numpy as jnp
from jax import lax
from jax.sharding import PartitionSpec as P

D = 8192
BLOCK = 128
BETA_ONE = 0.965
BETA_TWO = 0.99
GAMMA_CLIP = 0.01
CONTRACT = (((0,), (0,)), ((), ()))


def expand_tiles(tile_grid, tile_width):
    return jnp.repeat(jnp.repeat(tile_grid, tile_width, axis=0), tile_width, axis=1).astype(
        jnp.float32
    )


def on_device(activations, cot_true, cot_sampled, tile_mask, moment, curvature):
    dp_count = lax.axis_size("dp")
    kv_cols = cot_true.shape[1]
    col_tiles = kv_cols // BLOCK
    row_count = D // dp_count
    tokens_all = activations.shape[0] * dp_count
    inv_tokens = 1.0 / tokens_all
    panel = lax.all_gather(activations, "mp", axis=1, tiled=True)
    cotangents = jnp.concatenate([cot_true, cot_sampled], axis=1)
    local_tiles = lax.dynamic_slice_in_dim(
        tile_mask, lax.axis_index("mp") * col_tiles, col_tiles, 1
    )
    owned_tiles = row_count // BLOCK
    first_tile = lax.axis_index("dp") * owned_tiles
    product = lax.dot_general(panel, cotangents, CONTRACT, preferred_element_type=jnp.float32)
    row_mask = expand_tiles(local_tiles, BLOCK)
    owned = lax.psum_scatter(
        product * inv_tokens * jnp.concatenate([row_mask, row_mask], axis=1),
        "dp",
        scatter_dimension=0,
        tiled=True,
    )
    owned_mask = expand_tiles(
        lax.dynamic_slice_in_dim(local_tiles, first_tile, owned_tiles, 0), BLOCK
    )
    grad_true = owned[:, :kv_cols]
    grad_sampled = owned[:, kv_cols:]
    moment_new = BETA_ONE * moment + (1.0 - BETA_ONE) * grad_true
    hessian = tokens_all * grad_sampled * grad_sampled
    curvature_next = BETA_TWO * curvature + (1.0 - BETA_TWO) * hessian
    update = jnp.clip(moment_new / (GAMMA_CLIP * curvature_next), -1.0, 1.0) * owned_mask
    return (update, curvature_next * owned_mask)


def solution(mesh):
    return jax.shard_map(
        on_device,
        mesh=mesh,
        in_specs=(P("dp", "mp"), P("dp", "mp"), P("dp", "mp"), P(), P("dp", "mp"), P("dp", "mp")),
        out_specs=(P("dp", "mp"), P("dp", "mp")),
        check_vma=False,
    )
```

profile of v0, /device:TPU:82, one launch (start us, length us, event | category | flops | bytes accessed | tf_op | source)
XLA Modules:
  0.0 553.9 jit_solution(4977731851931626802)
XLA Ops:
  7.2 0.0 all-gather.2.cloned.1.call-start
  7.2 0.7 all-gather.2.cloned.1.call-update
  7.9 0.0 reduce-scatter.2.cloned.1.call-start
  7.9 0.7 dynamic-slice_convert_fusion.1
  8.6 0.1 broadcast_bitcast_fusion
  8.7 0.1 copy.16
  8.8 151.7 %all-gather.2.cloned.1.call-done = bf16[1024,8192]{1,0:T(8,128)(2,1)} async-done(((bf16[1024,2048]{1,0:T(8,128)(2,1)}), bf16[1024,8192]{1,0:T(8,128)(2,1)}) %all-gather.2.cloned.1.call-update) | async-done | bytes 16777232 | tf_op jit(solution)/shard_map/all_gather | solution.py:27
  160.5 0.9 broadcast_in_dim.13
  161.4 16.2 %maximum_multiply_fusion = f32[8192,512]{0,1:T(8,128)} fusion(f32[8192,256]{0,1:T(8,128)S(1)} %bitcast.21, bf16[1024,8192]{1,0:T(8,128)(2,1)} %all-gather.2.cloned.1.call-done, bf16[1024,256]{1,0:T(8,128)(2,1)} %param.8, bf16[1024,256]{1,0:T(8,128)(2,1)} %param.7), kind=kOutput, calls=%fused_computation | convolution fusion | flops 8604614656 | bytes 42991616 | tf_op jit(solution)/shard_map/dot_general | solution.py:34
  177.6 0.0 copy-start
  177.6 0.0 copy-start.1
  177.6 0.0 reduce-scatter.2.cloned.1.call-update
  177.6 0.8 dynamic-slice_convert_fusion
  178.5 0.1 broadcast_bitcast_fusion.1
  178.5 0.0 copy-done
  178.6 0.1 copy.8
  178.7 0.0 copy-done.1
  178.7 0.1 copy.9
  178.8 365.4 %reduce-scatter.2.cloned.1.call-done = f32[256,512]{0,1:T(8,128)} async-done(((f32[8192,512]{0,1:T(8,128)}), f32[256,512]{0,1:T(8,128)}) %reduce-scatter.2.cloned.1.call-update) | async-done | bytes 524304 | tf_op jit(solution)/shard_map/reduce_scatter | solution.py:36
  544.2 1.2 bitcast_multiply_fusion
  545.4 0.8 copy.10
  546.2 0.8 copy.11
  (1 shorter events, 0.0 us)
Async XLA Ops:
  7.2 153.3 %all-gather.2.cloned.1.call-start = ((), (), s32[]{:S(2)}) async-start(), calls=%async_computation.1 | async-start | bytes 20971520 | tf_op jit(solution)/shard_map/all_gather | solution.py:27
  7.9 536.3 %reduce-scatter.2.cloned.1.call-start = ((), (), s32[]{:S(2)}) async-start(), calls=%async_computation.2 | async-start | bytes 17301504 | tf_op jit(solution)/shard_map/reduce_scatter | solution.py:36
  177.6 0.9 copy-start
  177.6 1.1 copy-start.1
Sparse Core Ops, SparseCore 0:
  9.6 150.8 all-gather.1
  177.8 366.4 reduce-scatter.1
where the time goes:
time: 554 us
  waiting for transfers between devices  518 us (94%)
  matrix products  16.2 us (3%)
  between operations  14.1 us (3%)
    reduce_scatter x1, waiting for transfers between devices, on_device(): lax.psum_scatter(product * inv_tokens * jnp.concatenate([row_mask, row_ma...  365 us
    all_gather x1, waiting for transfers between devices, on_device(): panel = lax.all_gather(activations, 'mp', axis=1, tiled=True)  152 us
    dot_general x1, matrix products, on_device(): lax.dot_general(panel, cotangents, CONTRACT, preferred_element_type=jnp.f...  16.2 us
  transfers between devices with their start and end apart: 2, of which 2 were waited for; matrix products, arithmetic and copies ran while one was open for 0% of the time, Pallas kernels for 0%

commit v1 on v0

--- a/solution.py
+++ b/solution.py
@@ -24,7 +24,9 @@
     row_count = D // dp_count
     tokens_all = activations.shape[0] * dp_count
     inv_tokens = 1.0 / tokens_all
-    panel = lax.all_gather(activations, "mp", axis=1, tiled=True)
+    panel = jnp.concatenate(
+        lax.all_to_all(jnp.stack([activations] * lax.axis_size("mp")), "mp", 0, 0), axis=1
+    )
     cotangents = jnp.concatenate([cot_true, cot_sampled], axis=1)
     local_tiles = lax.dynamic_slice_in_dim(
         tile_mask, lax.axis_index("mp") * col_tiles, col_tiles, 1

time: 554 us -> 612 us (1.10)
  waiting for transfers between devices: 518 us -> 547 us
  local copies, waits for them, and re-layouts: 3.09 us -> 20.9 us
  starting transfers between devices: 0.08 us -> 7.15 us
    all_to_all x0 -> x1, waiting for transfers between devices: none -> 183 us  [on_device(): lax.all_to_all(jnp.stack([activations] * lax.axis_size('mp')), 'mp', 0, 0)]
    all_gather x1 -> x0, waiting for transfers between devices: 152 us -> none  [on_device(): panel = lax.all_gather(activations, 'mp', axis=1, tiled=True)]
    another operation x0 -> x1, local copies, waits for them, and re-layouts: none -> 7.46 us  [on_device(): jnp.stack([activations] * lax.axis_size('mp'))]
    unnamed x12 -> x19, local copies, waits for them, and re-layouts: 2.16 us -> 9.3 us
    all_to_all x0 -> x1, starting transfers between devices: none -> 7.11 us  [on_device(): lax.all_to_all(jnp.stack([activations] * lax.axis_size('mp')), 'mp', 0, 0)]
where the time goes in v1:
time: 612 us
  waiting for transfers between devices  547 us (89%)
  matrix products  21.4 us (3%)
  local copies, waits for them, and re-layouts  20.9 us (3%)
  between operations  14.1 us (2%)
  starting transfers between devices  7.15 us (1%)
    reduce_scatter x1, waiting for transfers between devices, on_device(): lax.psum_scatter(product * inv_tokens * jnp.concatenate([row_mask, row_ma...  364 us
    all_to_all x1, waiting for transfers between devices, on_device(): lax.all_to_all(jnp.stack([activations] * lax.axis_size('mp')), 'mp', 0, 0)  183 us
    dot_general x1, matrix products, on_device(): lax.dot_general(panel, cotangents, CONTRACT, preferred_element_type=jnp.f...  21.4 us
  transfers between devices with their start and end apart: 2, of which 2 were waited for; matrix products, arithmetic and copies ran while one was open for 0% of the time, Pallas kernels for 0%

profile of v1, /device:TPU:82, one launch (start us, length us, event | category | flops | bytes accessed | tf_op | source)
XLA Modules:
  0.0 611.9 jit_solution(14547119893580252377)
XLA Ops:
  7.2 6.4 %copy.13 = bf16[1024,2048]{0,1:T(8,128)(2,1)} copy(bf16[1024,2048]{1,0:T(8,128)(2,1)} %param.6) | data formatting | bytes 8388608 | tf_op args[0]
  13.6 7.5 %stack.2 = bf16[4,1024,2048]{1,2,0:T(8,128)(2,1)} broadcast(bf16[1024,2048]{0,1:T(8,128)(2,1)} %copy.13), dimensions={1,2} | broadcast | bytes 20971520 | tf_op jit(solution)/shard_map/stack | solution.py:28
  21.0 0.0 copy-start.2
  21.0 0.0 copy-start.3
  21.0 0.0 copy-start.4
  21.0 7.1 %all-to-all-start = ((bf16[4,1024,2048]{1,2,0:T(8,128)(2,1)}), bf16[4,1024,2048]{1,2,0:T(8,128)(2,1)}, u32[]{:S(2)}, u32[]{:S(2)}) async-start(bf16[4,1024,2048]{1,2,0:T(8,128)(2,1)} %stack.2), calls=%async_computation | async-start | bytes 33554432 | tf_op jit(solution)/shard_map/all_to_all | solution.py:28
  28.1 0.0 reduce-scatter.2.cloned.1.call-start
  28.2 0.0 copy-done.2
  28.2 0.1 broadcast_bitcast_fusion
  28.3 0.1 copy.21
  28.4 182.8 %all-to-all-done = bf16[4,1024,2048]{1,2,0:T(8,128)(2,1)} async-done(((bf16[4,1024,2048]{1,2,0:T(8,128)(2,1)}), bf16[4,1024,2048]{1,2,0:T(8,128)(2,1)}, u32[]{:S(2)}, u32[]{:S(2)}) %all-to-all-start) | async-done | bytes 16777248 | tf_op jit(solution)/shard_map/all_to_all | solution.py:28
  211.2 4.2 broadcast_in_dim.13
  215.3 0.0 copy-done.3
  215.3 0.0 copy-done.4
  215.3 21.4 %maximum_multiply_fusion = f32[8192,512]{0,1:T(8,128)} fusion(f32[8192,256]{0,1:T(8,128)} %bitcast.24, bf16[1024,8192]{0,1:T(8,128)(2,1)} %bitcast.1, bf16[1024,256]{1,0:T(8,128)(2,1)S(1)} %copy-done.3, bf16[1024,256]{1,0:T(8,128)(2,1)S(1)} %copy-done.4), kind=kOutput, calls=%fused_computation | convolution fusion | flops 8604614656 | bytes 42991616 | tf_op jit(solution)/shard_map/dot_general | solution.py:36
  236.7 0.0 copy-start
  236.7 0.0 copy-start.1
  236.7 0.0 reduce-scatter.2.cloned.1.call-update
  236.8 0.1 dynamic-slice_convert_fusion
  236.8 0.1 broadcast_bitcast_fusion.1
  236.9 0.8 copy-done
  237.7 0.1 copy.12
  237.8 0.0 copy-done.1
  237.8 0.1 copy.14
  237.9 364.3 %reduce-scatter.2.cloned.1.call-done = f32[256,512]{0,1:T(8,128)} async-done(((f32[8192,512]{0,1:T(8,128)}), f32[256,512]{0,1:T(8,128)}) %reduce-scatter.2.cloned.1.call-update) | async-done | bytes 524304 | tf_op jit(solution)/shard_map/reduce_scatter | solution.py:38
  602.2 1.2 bitcast_multiply_fusion
  603.4 0.8 copy.15
  604.2 0.8 copy.16
  (2 shorter events, 0.0 us)
Async XLA Ops:
  21.0 7.2 %copy-start.2 = (s32[64,8]{0,1:T(8,128)S(1)}, s32[64,8]{0,1:T(8,128)}, u32[]{:S(2)}) copy-start(s32[64,8]{0,1:T(8,128)} %param.9) | copy-start | bytes 6148
  21.0 194.3 %copy-start.3 = (bf16[1024,256]{1,0:T(8,128)(2,1)S(1)}, bf16[1024,256]{1,0:T(8,128)(2,1)}, u32[]{:S(2)}) copy-start(bf16[1024,256]{1,0:T(8,128)(2,1)} %param.8) | copy-start | bytes 1572868
  21.0 194.3 %copy-start.4 = (bf16[1024,256]{1,0:T(8,128)(2,1)S(1)}, bf16[1024,256]{1,0:T(8,128)(2,1)}, u32[]{:S(2)}) copy-start(bf16[1024,256]{1,0:T(8,128)(2,1)} %param.7) | copy-start | bytes 1572868
  21.0 190.1 %all-to-all-start = ((bf16[4,1024,2048]{1,2,0:T(8,128)(2,1)}), bf16[4,1024,2048]{1,2,0:T(8,128)(2,1)}, u32[]{:S(2)}, u32[]{:S(2)}) async-start(bf16[4,1024,2048]{1,2,0:T(8,128)(2,1)} %stack.2), calls=%async_computation | async-start | bytes 33554432 | tf_op jit(solution)/shard_map/all_to_all | solution.py:28
  28.1 574.1 %reduce-scatter.2.cloned.1.call-start = ((), (), s32[]{:S(2)}) async-start(), calls=%async_computation.2 | async-start | bytes 17301504 | tf_op jit(solution)/shard_map/reduce_scatter | solution.py:38
  236.7 0.9 copy-start
  236.7 1.1 copy-start.1
Sparse Core Ops, SparseCore 0:
  236.9 365.2 reduce-scatter.1
